TPU v7x, 32 devices: a whole 2x2x4 slice. The times are simulated.
32 devices in a mesh: dom: 2 (over y), dp: 16 (over z, x, core).
Axes of the slice: x: 2, y: 2, z: 4, core: 2. Of those that a mesh axis runs over, the one named last changes fastest.
Arguments:
- positions: float32 [1024, 128], P(('dom', 'dp')), may hold values from -6 to 6
- length_scale: float32 [1], replicated, may hold values from 16 to 128
- features: float32 [32768, 128], P('dp'), may hold values from -0.5 to 0.5
- labels: int32 [32768], P('dp'), may hold values 0 or 1
- batch_index: int32 [8192], P('dp'), may hold values from 0 to 2047
Outputs:
- moved: float32 [1024, 128], P(('dom', 'dp'))
- score: float32 [1024, 128], P(('dom', 'dp'))
Inputs may be any that keep to these rules, and one draw needn't show every extreme that they name: `batch_index`: an index into the 2048 feature rows of the same dp index.
All inputs are finite; a program needn't handle non-finite values. No bound on the sum of `labels` on one device may be relied on, other than what follows from the above.
Results may differ from a plain program's by a relative error of at most 0.0001.
Values sent between devices are 32-bit elements; how exact they have to be, the bound alone decides.
No kernel may reach another device: no remote copies, remote signals or barrier semaphores. Data moves between devices by JAX's collectives and lax.ppermute only.
A program may use at most 64 MiB of HBM per device.

v0:
```python
import math
import jax
import jax.numpy as jnp
from jax import lax
from jax.sharding import PartitionSpec as P

STEPS = 2
HIGH = lax.Precision.HIGHEST
STEP_SIZE = 2.0


def likelihood(block, rows, targets, scale):
    logits = jnp.dot(block, rows.T, precision=HIGH, preferred_element_type=jnp.float32)
    resid = targets[None, :] - jax.nn.sigmoid(logits)
    return jnp.dot(resid, rows, precision=HIGH, preferred_element_type=jnp.float32) * scale


def displace(aimed, sources, source_score, spread):
    square_a = jnp.sum(aimed * aimed, axis=1)
    square_b = jnp.sum(sources * sources, axis=1)
    inner = jnp.dot(aimed, sources.T, precision=HIGH, preferred_element_type=jnp.float32)
    dist = square_a[:, None] + square_b[None, :] - 2.0 * inner
    kernel = lax.rsqrt(1.0 + dist / spread)
    cubed = kernel * kernel * kernel
    drive = jnp.dot(kernel, source_score, precision=HIGH, preferred_element_type=jnp.float32)
    pulled = jnp.dot(cubed, sources, precision=HIGH, preferred_element_type=jnp.float32)
    return drive + (aimed * jnp.sum(cubed, axis=1)[:, None] - pulled) / spread


def shards(positions, length_scale, features, labels, batch_index):
    rows = features[batch_index]
    targets = labels[batch_index].astype(jnp.float32)
    scale = 1.0 / math.sqrt(batch_index.shape[0] * lax.axis_size("dp"))
    spread = length_scale[0]
    local_count = positions.shape[0]
    particle_total = local_count * lax.axis_size("dom") * lax.axis_size("dp")
    factor = STEP_SIZE / particle_total
    current = positions
    score = positions
    for iteration in range(STEPS):
        block = lax.all_gather(current, "dp", axis=0, tiled=True)
        gradient_block = lax.psum(likelihood(block, rows, targets, scale), "dp")
        score_block = gradient_block - block
        place = lax.axis_index("dp") * local_count
        score = lax.dynamic_slice_in_dim(score_block, place, local_count, 0)
        aimed_all = lax.all_gather(current, "dom", axis=0, tiled=True)
        moves = lax.psum_scatter(
            displace(aimed_all, block, score_block, spread), "dom", scatter_dimension=0, tiled=True
        )
        current = current + factor * moves
    return (current, score)


def solution(mesh):
    placed = (P(("dom", "dp"), None), P(), P("dp", None), P("dp"), P("dp"))
    return jax.shard_map(
        shards,
        mesh=mesh,
        in_specs=placed,
        out_specs=(P(("dom", "dp"), None), P(("dom", "dp"), None)),
        check_vma=False,
    )
```

profile of v0, /device:TPU:0, one launch (start us, length us, event | category | flops | bytes accessed | tf_op | source)
XLA Modules:
  0.0 272.5 jit_solution(17130246005774058776)
XLA Ops:
  7.2 0.0 copy-start
  7.2 0.0 copy-start.3
  7.2 0.0 all-reduce.3.cloned.1.call-start
  7.2 24.2 %all_gather.13 = f32[512,128]{1,0:T(8,128)S(1)} all-gather(f32[32,128]{1,0:T(8,128)} %param.5), channel_id=1, replica_groups=mesh['dom'=2,'dp'=16] {'dp'}, dimensions={0}, use_global_device_ids=true | all-gather | bytes 278528 | tf_op jit(solution)/shard_map/all_gather | solution.py:41
  31.4 0.0 copy-done.3
  31.4 0.0 copy-done
  31.4 0.0 copy-start.1
  31.5 1.0 gather_fusion.1
  32.5 0.0 copy-done.1
  32.5 3.1 %gather_fusion = s32[512]{0:T(512)S(1)} fusion(s32[2048]{0:T(1024)S(1)} %copy-done.1, s32[1024]{0:T(1024)S(1)} %pad_clamp_fusion), kind=kCustom, calls=%fused_computation | custom fusion | bytes 6144 | tf_op jit(solution)/shard_map/gather | solution.py:32
  35.7 1.1 fusion.4
  36.8 2.5 convolution_multiply_fusion.1
  39.4 0.0 all-reduce.3.cloned.1.call-update
  39.4 0.0 copy-start.2
  39.4 0.0 reduce-scatter.3.cloned.1.call-start
  39.4 0.1 multiply_reduce_fusion.1
  39.6 0.5 copy-done.2
  40.1 4.4 %all_gather.12 = f32[64,128]{1,0:T(8,128)S(1)} all-gather(f32[32,128]{1,0:T(8,128)S(1)} %copy-done.2), channel_id=1, replica_groups=mesh['dom'=2,'dp'=16] {'dom'}, dimensions={0}, use_global_device_ids=true | all-gather | bytes 49152 | tf_op jit(solution)/shard_map/all_gather | solution.py:46
  45.1 0.1 multiply_reduce_fusion.3
  45.3 0.5 fusion.22
  45.8 80.8 %all-reduce.3.cloned.1.call-done = f32[512,128]{1,0:T(8,128)} async-done(((f32[512,128]{1,0:T(8,128)}), f32[512,128]{1,0:T(8,128)}) %all-reduce.3.cloned.1.call-update) | async-done | bytes 262160 | tf_op jit(solution)/shard_map/psum | solution.py:42
  126.6 1.2 fusion.20
  127.8 0.9 fusion.19
  128.7 0.0 reduce-scatter.3.cloned.1.call-update
  128.8 0.0 all-reduce.5.cloned.1.call-start
  128.8 10.6 %reduce-scatter.3.cloned.1.call-done = f32[32,128]{1,0:T(8,128)} async-done(((f32[64,128]{1,0:T(8,128)}), f32[32,128]{1,0:T(8,128)}) %reduce-scatter.3.cloned.1.call-update) | async-done | bytes 16400 | tf_op jit(solution)/shard_map/reduce_scatter | solution.py:47
  139.4 0.7 multiply_add_fusion.1
  140.1 22.0 %all_gather.15 = f32[512,128]{1,0:T(8,128)S(1)} all-gather(f32[32,128]{1,0:T(8,128)S(1)} %multiply_add_fusion.1), channel_id=1, replica_groups=mesh['dom'=2,'dp'=16] {'dp'}, dimensions={0}, use_global_device_ids=true | all-gather | bytes 278528 | tf_op jit(solution)/shard_map/all_gather | solution.py:41
  162.1 1.1 fusion.7
  163.2 1.7 convolution_multiply_fusion
  164.9 0.0 all-reduce.5.cloned.1.call-update
  164.9 0.0 reduce-scatter.5.cloned.1.call-start
  165.0 4.4 %all_gather.14 = f32[64,128]{1,0:T(8,128)S(1)} all-gather(f32[32,128]{1,0:T(8,128)S(1)} %multiply_add_fusion.1), channel_id=1, replica_groups=mesh['dom'=2,'dp'=16] {'dom'}, dimensions={0}, use_global_device_ids=true | all-gather | bytes 49152 | tf_op jit(solution)/shard_map/all_gather | solution.py:46
  169.4 0.1 multiply_reduce_fusion.2
  169.5 81.7 %all-reduce.5.cloned.1.call-done = f32[512,128]{1,0:T(8,128)} async-done(((f32[512,128]{1,0:T(8,128)}), f32[512,128]{1,0:T(8,128)}) %all-reduce.5.cloned.1.call-update) | async-done | bytes 262160 | tf_op jit(solution)/shard_map/psum | solution.py:42
  251.2 1.1 fusion.24
  252.3 0.5 fusion.23
  252.8 0.3 fusion.25
  253.1 0.9 fusion.17
  254.0 0.0 reduce-scatter.5.cloned.1.call-update
  254.0 0.6 constant_dynamic-slice_fusion
  254.6 10.0 %reduce-scatter.5.cloned.1.call-done = f32[32,128]{1,0:T(8,128)} async-done(((f32[64,128]{1,0:T(8,128)}), f32[32,128]{1,0:T(8,128)}) %reduce-scatter.5.cloned.1.call-update) | async-done | bytes 16400 | tf_op jit(solution)/shard_map/reduce_scatter | solution.py:47
  264.6 1.3 multiply_add_fusion
  (3 shorter events, 0.0 us)
Async XLA Ops:
  7.2 24.3 %copy-start = (f32[2048,128]{1,0:T(8,128)S(1)}, f32[2048,128]{1,0:T(8,128)}, u32[]{:S(2)}) copy-start(f32[2048,128]{1,0:T(8,128)} %param.7) | copy-start | bytes 3145732
  7.2 24.2 %copy-start.3 = (s32[512]{0:T(512)S(1)}, s32[512]{0:T(512)}, u32[]{:S(2)}) copy-start(s32[512]{0:T(512)} %param.9) | copy-start | bytes 6148
  7.2 119.4 %all-reduce.3.cloned.1.call-start = ((), (), s32[]{:S(2)}) async-start(), calls=%async_computation.2 | async-start | bytes 524288 | tf_op jit(solution)/shard_map/psum | solution.py:42
  31.4 1.1 copy-start.1
  39.4 0.7 copy-start.2
  39.4 100.0 %reduce-scatter.3.cloned.1.call-start = ((), (), s32[]{:S(2)}) async-start(), calls=%async_computation.3 | async-start | bytes 49152 | tf_op jit(solution)/shard_map/reduce_scatter | solution.py:47
  128.8 122.4 %all-reduce.5.cloned.1.call-start = ((), (), s32[]{:S(2)}) async-start(), calls=%async_computation.4 | async-start | bytes 524288 | tf_op jit(solution)/shard_map/psum | solution.py:42
  164.9 99.7 %reduce-scatter.5.cloned.1.call-start = ((), (), s32[]{:S(2)}) async-start(), calls=%async_computation.5 | async-start | bytes 49152 | tf_op jit(solution)/shard_map/reduce_scatter | solution.py:47
Sparse Core Ops, SparseCore 0:
  39.5 87.0 all-reduce.2
  128.9 10.4 reduce-scatter.2
  165.1 86.0 all-reduce.4
  254.1 10.4 reduce-scatter.4
where the time goes:
time: 273 us
  waiting for transfers between devices  183 us (67%)
  blocking collectives  55 us (20%)
  between operations  14.5 us (5%)
  matrix products  10.8 us (4%)
  local copies, waits for them, and re-layouts  5.33 us (2%)
  other arithmetic  3.51 us (1%)
    psum x2, waiting for transfers between devices, shards(): gradient_block = lax.psum(likelihood(block, rows, targets, scale), 'dp')  163 us
    all_gather x2, blocking collectives, shards(): block = lax.all_gather(current, 'dp', axis=0, tiled=True)  46.2 us
    reduce_scatter x2, waiting for transfers between devices, shards(): lax.psum_scatter(displace(aimed_all, block, score_block, spread), 'dom',...  20.6 us
    all_gather x2, blocking collectives, shards(): aimed_all = lax.all_gather(current, 'dom', axis=0, tiled=True)  8.8 us
  transfers between devices with their start and end apart: 4, of which 4 were waited for; matrix products, arithmetic and copies ran while one was open for 1% of the time, Pallas kernels for 0%

commit v1 on v0

--- a/solution.py
+++ b/solution.py
@@ -39,7 +39,9 @@
     score = positions
     for iteration in range(STEPS):
         block = lax.all_gather(current, "dp", axis=0, tiled=True)
-        gradient_block = lax.psum(likelihood(block, rows, targets, scale), "dp")
+        gradient_block = jnp.sum(
+            lax.all_gather(likelihood(block, rows, targets, scale), "dp"), axis=0
+        )
         score_block = gradient_block - block
         place = lax.axis_index("dp") * local_count
         score = lax.dynamic_slice_in_dim(score_block, place, local_count, 0)

time: 273 us -> 194 us (0.71)
  waiting for transfers between devices: 183 us -> 101 us
  other arithmetic: 3.51 us -> 8.06 us
    psum x2 -> x0, waiting for transfers between devices: 163 us -> none  [shards(): gradient_block = lax.psum(likelihood(block, rows, targets, scale), 'dp')]
    all_gather x0 -> x2, waiting for transfers between devices: none -> 84.2 us  [shards(): lax.all_gather(likelihood(block, rows, targets, scale), 'dp')]
    reduce_sum x0 -> x2, other arithmetic: none -> 4.81 us  [shards(): jnp.sum(lax.all_gather(likelihood(block, rows, targets, scale), 'dp'), ax...]
    reduce_scatter x2, waiting for transfers between devices: 20.6 us -> 16.6 us  [shards(): lax.psum_scatter(displace(aimed_all, block, score_block, spread), 'dom',...]
where the time goes in v1:
time: 194 us
  waiting for transfers between devices  101 us (52%)
  blocking collectives  55 us (28%)
  between operations  14.5 us (7%)
  matrix products  9.86 us (5%)
  other arithmetic  8.06 us (4%)
  local copies, waits for them, and re-layouts  5.05 us (3%)
    all_gather x2, waiting for transfers between devices, shards(): lax.all_gather(likelihood(block, rows, targets, scale), 'dp')  84.2 us
    all_gather x2, blocking collectives, shards(): block = lax.all_gather(current, 'dp', axis=0, tiled=True)  46.2 us
    reduce_scatter x2, waiting for transfers between devices, shards(): lax.psum_scatter(displace(aimed_all, block, score_block, spread), 'dom',...  16.6 us
    all_gather x2, blocking collectives, shards(): aimed_all = lax.all_gather(current, 'dom', axis=0, tiled=True)  8.81 us
    reduce_sum x2, other arithmetic, shards(): jnp.sum(lax.all_gather(likelihood(block, rows, targets, scale), 'dp'), ax...  4.81 us
    dot_general x2, matrix products, likelihood(): jnp.dot(resid, rows, precision=HIGH, preferred_element_type=jnp.float32)  4.2 us
  transfers between devices with their start and end apart: 4, of which 4 were waited for; matrix products, arithmetic and copies ran while one was open for 1% of the time, Pallas kernels for 0%

profile of v1, /device:TPU:0, one launch (start us, length us, event | category | flops | bytes accessed | tf_op | source)
XLA Modules:
  0.0 193.5 jit_solution(2082215944158865842)
XLA Ops:
  7.2 0.0 copy-start
  7.2 0.0 all-gather.5.cloned.1.call-start
  7.2 24.2 %all_gather.25 = f32[512,128]{1,0:T(8,128)S(1)} all-gather(f32[32,128]{1,0:T(8,128)} %param.5), channel_id=1, replica_groups=mesh['dom'=2,'dp'=16] {'dp'}, dimensions={0}, use_global_device_ids=true | all-gather | bytes 278528 | tf_op jit(solution)/shard_map/all_gather | solution.py:41
  31.4 0.7 compare_select_fusion
  32.1 0.0 copy-done
  32.1 1.0 gather_fusion.1
  33.1 0.0 copy-start.1
  33.2 3.4 %gather_fusion = s32[512]{0:T(512)S(1)} fusion(s32[2048]{0:T(1024)} %param.8, s32[1024]{0:T(1024)S(1)} %pad_clamp_fusion), kind=kCustom, calls=%fused_computation | custom fusion | bytes 6144 | tf_op jit(solution)/shard_map/gather | solution.py:32
  36.6 1.1 fusion.4
  37.7 2.5 %convolution_multiply_fusion.1 = f32[512,128]{1,0:T(8,128)} fusion(f32[512,512]{1,0:T(8,128)S(1)} %fusion.4, f32[512,128]{1,0:T(8,128)S(1)} %gather_fusion.1), kind=kOutput, calls=%fused_computation.13 | convolution fusion | flops 402718720 | bytes 1572864 | tf_op jit(solution)/shard_map/dot_general | solution.py:15
  40.2 0.0 all-gather.5.cloned.1.call-update
  40.2 0.0 reduce-scatter.3.cloned.1.call-start
  40.9 0.0 copy-done.1
  41.0 4.4 %all_gather.24 = f32[64,128]{1,0:T(8,128)S(1)} all-gather(f32[32,128]{1,0:T(8,128)S(1)} %copy-done.1), channel_id=1, replica_groups=mesh['dom'=2,'dp'=16] {'dom'}, dimensions={0}, use_global_device_ids=true | all-gather | bytes 49152 | tf_op jit(solution)/shard_map/all_gather | solution.py:48
  45.4 0.1 multiply_reduce_fusion.3
  45.5 0.2 multiply_reduce_fusion.1
  45.6 0.5 fusion.22
  46.1 41.9 %all-gather.5.cloned.1.call-done = f32[8192,128]{1,0:T(8,128)} async-done(((f32[512,128]{1,0:T(8,128)}), f32[8192,128]{1,0:T(8,128)}) %all-gather.5.cloned.1.call-update) | async-done | bytes 4194320 | tf_op jit(solution)/shard_map/all_gather | solution.py:43
  88.1 2.4 %reduce_sum.74 = f32[512,128]{1,0:T(8,128)S(1)} reduce(f32[16,512,128]{2,1,0:T(8,128)} %bitcast.25, f32[]{:T(128)} %constant.10.clone.1), dimensions={0}, to_apply=%region_2.0 | reduce | flops 983040 | bytes 4456452 | tf_op jit(solution)/shard_map/reduce_sum | solution.py:42
  90.5 0.3 fusion.20
  90.8 0.9 fusion.19
  91.7 0.0 reduce-scatter.3.cloned.1.call-update
  91.7 0.0 all-gather.7.cloned.1.call-start
  91.7 8.6 %reduce-scatter.3.cloned.1.call-done = f32[32,128]{1,0:T(8,128)} async-done(((f32[64,128]{1,0:T(8,128)}), f32[32,128]{1,0:T(8,128)}) %reduce-scatter.3.cloned.1.call-update) | async-done | bytes 16400 | tf_op jit(solution)/shard_map/reduce_scatter | solution.py:49
  100.3 0.7 multiply_add_fusion.1
  101.1 22.0 %all_gather.29 = f32[512,128]{1,0:T(8,128)S(1)} all-gather(f32[32,128]{1,0:T(8,128)S(1)} %multiply_add_fusion.1), channel_id=1, replica_groups=mesh['dom'=2,'dp'=16] {'dp'}, dimensions={0}, use_global_device_ids=true | all-gather | bytes 278528 | tf_op jit(solution)/shard_map/all_gather | solution.py:41
  123.1 1.1 fusion.7
  124.2 1.7 convolution_multiply_fusion
  125.9 0.0 all-gather.7.cloned.1.call-update
  125.9 0.0 reduce-scatter.5.cloned.1.call-start
  126.0 4.4 %all_gather.28 = f32[64,128]{1,0:T(8,128)S(1)} all-gather(f32[32,128]{1,0:T(8,128)S(1)} %multiply_add_fusion.1), channel_id=1, replica_groups=mesh['dom'=2,'dp'=16] {'dom'}, dimensions={0}, use_global_device_ids=true | all-gather | bytes 49152 | tf_op jit(solution)/shard_map/all_gather | solution.py:48
  130.4 0.1 multiply_reduce_fusion.2
  130.5 42.3 %all-gather.7.cloned.1.call-done = f32[8192,128]{1,0:T(8,128)} async-done(((f32[512,128]{1,0:T(8,128)}), f32[8192,128]{1,0:T(8,128)}) %all-gather.7.cloned.1.call-update) | async-done | bytes 4194320 | tf_op jit(solution)/shard_map/all_gather | solution.py:43
  172.7 2.4 %reduce_sum.78 = f32[512,128]{1,0:T(8,128)S(1)} reduce(f32[16,512,128]{2,1,0:T(8,128)} %bitcast.24, f32[]{:T(128)} %constant.10.clone.1), dimensions={0}, to_apply=%region_7.0 | reduce | flops 983040 | bytes 4456452 | tf_op jit(solution)/shard_map/reduce_sum | solution.py:42
  175.1 0.1 fusion.24
  175.3 0.5 fusion.23
  175.8 0.3 fusion.25
  176.1 0.9 fusion.17
  177.0 0.0 reduce-scatter.5.cloned.1.call-update
  177.0 0.6 constant_dynamic-slice_fusion
  177.6 8.0 %reduce-scatter.5.cloned.1.call-done = f32[32,128]{1,0:T(8,128)} async-done(((f32[64,128]{1,0:T(8,128)}), f32[32,128]{1,0:T(8,128)}) %reduce-scatter.5.cloned.1.call-update) | async-done | bytes 16400 | tf_op jit(solution)/shard_map/reduce_scatter | solution.py:49
  185.7 1.3 multiply_add_fusion
  (2 shorter events, 0.0 us)
Async XLA Ops:
  7.2 24.9 %copy-start = (f32[2048,128]{1,0:T(8,128)S(1)}, f32[2048,128]{1,0:T(8,128)}, u32[]{:S(2)}) copy-start(f32[2048,128]{1,0:T(8,128)} %param.7) | copy-start | bytes 3145732
  7.2 80.9 %all-gather.5.cloned.1.call-start = ((), (), s32[]{:S(2)}) async-start(), calls=%async_computation.4 | async-start | bytes 4456448 | tf_op jit(solution)/shard_map/all_gather | solution.py:43
  33.1 7.8 %copy-start.1 = (f32[32,128]{1,0:T(8,128)S(1)}, f32[32,128]{1,0:T(8,128)}, u32[]{:S(2)}) copy-start(f32[32,128]{1,0:T(8,128)} %param.5) | copy-start | bytes 49156
  40.2 60.1 %reduce-scatter.3.cloned.1.call-start = ((), (), s32[]{:S(2)}) async-start(), calls=%async_computation.2 | async-start | bytes 49152 | tf_op jit(solution)/shard_map/reduce_scatter | solution.py:49
  91.7 81.1 %all-gather.7.cloned.1.call-start = ((), (), s32[]{:S(2)}) async-start(), calls=%async_computation.5 | async-start | bytes 4456448 | tf_op jit(solution)/shard_map/all_gather | solution.py:43
  125.9 59.8 %reduce-scatter.5.cloned.1.call-start = ((), (), s32[]{:S(2)}) async-start(), calls=%async_computation.3 | async-start | bytes 49152 | tf_op jit(solution)/shard_map/reduce_scatter | solution.py:49
Sparse Core Ops, SparseCore 0:
  40.4 47.6 all-gather.4
  91.8 8.4 reduce-scatter.2
  126.0 46.6 all-gather.6
  177.1 8.4 reduce-scatter.4
